TPU v7x, 32 devices: a whole 2x2x4 slice. The times are simulated.
32 devices in a mesh: group: 8 (over y, x, core), blk: 4 (over z).
Axes of the slice: x: 2, y: 2, z: 4, core: 2. Of those that a mesh axis runs over, the one named last changes fastest.
Arguments:
- front: float32 [8, 8192, 512], P('group', None, 'blk'), as said below
- child_blocks: float32 [8, 4, 8, 2, 128, 128], P('group', 'blk'), may hold values from -6 to 6
- child_rows: int32 [8, 4, 8, 2, 128], P('group', 'blk'), may hold values from 512 to 8191, as said below
- child_cols: int32 [8, 4, 8, 2, 128], P('group', 'blk'), may hold values from 0 to 127, each once within a row
- child_counts: int32 [8, 4, 8], P('group', 'blk'), may hold values from 0 to 2, as said below
Outputs:
- factors: float32 [8, 8192, 512], P('group', None, 'blk')
- pivots: float32 [8, 256], P('group')
Inputs may be any that keep to these rules, and one draw needn't show every extreme that they name: Rows 0 to 511 of each front form a symmetric matrix whose leading 2 * 128 rows and columns have a positive diagonal that dominates every row of that block; rows from 512 on are unstructured. `child_rows`: the 128 row indices of one slot are distinct and lie at or below row 512. `child_counts`: for every column block some destination group receives 2 live slots from every source group.
All inputs are finite; a program needn't handle non-finite values.
Results may differ from a plain program's by a relative error of at most 0.0003.
Values sent between devices are 32-bit elements; how exact they have to be, the bound alone decides.
No kernel may reach another device: no remote copies, remote signals or barrier semaphores. Data moves between devices by JAX's collectives and lax.ppermute only.
A program may use at most 64 MiB of HBM per device.

v0:
```python
import jax
import jax.numpy as jnp
from jax import lax
from jax.sharding import PartitionSpec as P

PANELS = 2


def from_root(x, axis, root):
    mine = lax.axis_index(axis) == root
    return lax.psum(jnp.where(mine, x, jnp.zeros_like(x)), axis)


def factor_panel(column, start):
    size = column.shape[1]
    square = lax.slice_in_dim(column, start, start + size, axis=0)
    lower_factor = jnp.linalg.cholesky(square)
    diag_root = jnp.diagonal(lower_factor)
    solved = lax.linalg.triangular_solve(
        lower_factor, column, left_side=False, lower=True, transpose_a=True
    )
    solved = solved / diag_root
    row_ids = lax.broadcasted_iota(jnp.int32, solved.shape, 0)
    solved = jnp.where(row_ids >= start, solved, jnp.zeros_like(solved))
    return (solved, diag_root * diag_root)


def per_device(front, child_blocks, child_rows, child_cols, child_counts):
    blocks_in, rows_in, cols_in, counts_in = (
        lax.all_to_all(child_blocks, "group", split_axis=2, concat_axis=0, tiled=True),
        lax.all_to_all(child_rows, "group", split_axis=2, concat_axis=0, tiled=True),
        lax.all_to_all(child_cols, "group", split_axis=2, concat_axis=0, tiled=True),
        lax.all_to_all(child_counts, "group", split_axis=2, concat_axis=0, tiled=True),
    )
    groups = blocks_in.shape[0]
    slots = blocks_in.shape[3]
    width = blocks_in.shape[4]
    flat_blocks = blocks_in.reshape(groups * slots, width, width)
    flat_rows = rows_in.reshape(groups * slots * width)
    flat_cols = cols_in.reshape(groups * slots, width)
    slot_ids = lax.broadcasted_iota(jnp.int32, (groups, slots), 1)
    live = (slot_ids < counts_in.reshape(groups, 1)).reshape(groups * slots)
    masked = jnp.where(live[:, None, None], flat_blocks, jnp.zeros_like(flat_blocks))
    target_ids = lax.broadcasted_iota(jnp.int32, (groups * slots, width, width), 2)
    placement = (flat_cols[:, :, None] == target_ids).astype(jnp.float32)
    placed = jnp.einsum("sij,sjc->sic", masked, placement, precision=lax.Precision.HIGHEST)
    assembled = front[0].at[flat_rows].add(placed.reshape(groups * slots * width, width))
    my_index = lax.axis_index("blk")
    my_start = my_index * width
    pivot_list = []
    for panel in range(PANELS):
        start = panel * width

        def own_factor(column):
            return factor_panel(column, start)

        def empty_factor(column):
            return (jnp.zeros_like(column), jnp.zeros((width,), jnp.float32))

        factor, pivot = lax.cond(my_index == panel, own_factor, empty_factor, assembled)
        factor, pivot = (from_root(factor, "blk", panel), from_root(pivot, "blk", panel))
        my_rows = lax.dynamic_slice_in_dim(factor, my_start, width, 0)
        updated = assembled - jnp.dot(factor * pivot, my_rows.T, precision=lax.Precision.HIGHEST)
        assembled = jnp.where(
            my_index == panel, factor, jnp.where(my_index > panel, updated, assembled)
        )
        pivot_list.append(pivot)
    return (assembled[None], jnp.concatenate(pivot_list)[None])


def solution(mesh):
    in_specs = (
        P("group", None, "blk"),
        P("group", "blk", None, None, None, None),
        P("group", "blk", None, None, None),
        P("group", "blk", None, None, None),
        P("group", "blk", None),
    )
    out_specs = (P("group", None, "blk"), P("group", None))
    return jax.shard_map(
        per_device, mesh=mesh, in_specs=in_specs, out_specs=out_specs, check_vma=False
    )
```

profile of v0, /device:TPU:0, one launch (start us, length us, event | category | flops | bytes accessed | tf_op | source)
XLA Modules:
  0.0 499.8 jit_solution(10520679641883010009)
XLA Ops:
  7.2 4.5 copy.57
  11.7 9.7 %all_to_all.16 = s32[1,1,8]{1,0,2:T(1,128)S(1)} all-to-all(s32[1,1,8]{1,0,2:T(1,128)S(1)} %copy.32), channel_id=1, replica_groups=mesh['group'=8,'blk'=4] {'group'}, dimensions={2} | all-to-all | bytes 64 | tf_op jit(solution)/shard_map/all_to_all | solution.py:33
  21.4 7.1 %all_to_all.17 = s32[1,1,8,2,128]{4,3,1,0,2:T(2,128)S(1)} all-to-all(s32[1,1,8,2,128]{4,3,1,0,2:T(2,128)S(1)} %bitcast.53), channel_id=1, replica_groups=mesh['group'=8,'blk'=4] {'group'}, dimensions={2} | all-to-all | bytes 16384 | tf_op jit(solution)/shard_map/all_to_all | solution.py:31
  28.5 3.6 all-to-all-start.2
  32.5 14.9 %all-to-all-done.2 = f32[1,1,8,2,128,128]{5,4,3,1,0,2:T(8,128)S(1)} async-done(((f32[1,1,8,2,128,128]{5,4,3,1,0,2:T(8,128)}), f32[1,1,8,2,128,128]{5,4,3,1,0,2:T(8,128)S(1)}, u32[]{:S(2)}, u32[]{:S(2)}) %all-to-all-start.2) | async-done | bytes 1048608 | tf_op jit(solution)/shard_map/all_to_all | solution.py:30
  47.4 3.3 all-to-all-start.3
  50.9 4.5 all-to-all-done.3
  56.4 14.5 %scatter_fusion = f32[8192,128]{1,0:T(8,128)} fusion(f32[8192,128]{1,0:T(8,128)} %bitcast.48, s32[2048]{0:T(1024)S(1)} %bitcast.50, f32[2048,128]{1,0:T(8,128)S(1)} %bitcast.49), kind=kCustom, calls=%fused_computation.2 | custom fusion | flops 262144 | bytes 3153920 | tf_op jit(solution)/shard_map/scatter-add | solution.py:47
  71.0 45.7 %conditional.2 = (f32[128]{0:T(128)S(1)}, f32[8192,128]{1,0:T(8,128)}) conditional(s32[]{:T(128)} %convert_element_type.8, () %tuple.27, (f32[8192,128]{1,0:T(8,128)}) %tuple.31), branch_computations={%region_1.2_spmd, %region_2.0_spmd} | conditional | flops 1611809536 | bytes 25957906 | solution.py:60
  71.0 5.6 %copy.41 = f32[8192,128]{0,1:T(8,128)} copy(f32[8192,128]{1,0:T(8,128)} %get-tuple-element.15) | data formatting | bytes 8388608 | tf_op jit(solution)/shard_map/scatter-add | solution.py:47
  78.4 11.7 %cholesky.44 = f32[128,128]{1,0:T(8,128)S(1)} custom-call(f32[128,128]{1,0:T(8,128)S(1)} %fusion.2), custom_call_target="Cholesky" | custom-call | tf_op jit(solution)/shard_map/cond/branch_1_fun/jit(cholesky)/cholesky | solution.py:17
  92.8 9.8 %custom-call.10 = f32[1,128,128]{1,2,0:T(8,128)S(1)} custom-call(f32[1,128,128]{2,1,0:T(8,128)S(1)} %get-tuple-element.18), custom_call_target="InvertDiagBlocksLowerTriangular" | custom-call | tf_op jit(solution)/shard_map/cond/branch_1_fun/triangular_solve/custom-call.0 | solution.py:19
  102.6 8.4 %fusion = f32[8192,128]{0,1:T(8,128)} fusion(f32[8192,128]{1,0:T(8,128)} %get-tuple-element.15, f32[128]{0:T(128)S(1)} %gather_fusion, f32[1,128,128]{1,2,0:T(8,128)S(1)} %custom-call.10), kind=kOutput, calls=%fused_computation.4 | convolution fusion | flops 1611661312 | bytes 8454656 | tf_op jit(solution)/shard_map/cond/branch_1_fun/triangular_solve/dot.3 | solution.py:19
  111.1 5.6 %copy.40 = f32[8192,128]{1,0:T(8,128)} copy(f32[8192,128]{0,1:T(8,128)} %fusion) | data formatting | bytes 8388608 | tf_op jit(solution)/shard_map/cond | solution.py:60
  116.7 4.4 broadcast_select_fusion.1
  121.1 9.0 %psum.29 = f32[128]{0:T(128)S(1)} all-reduce(f32[128]{0:T(128)S(1)} %broadcast_select_fusion.3), channel_id=1, replica_groups=mesh['group'=8,'blk'=4] {'blk'}, use_global_device_ids=true, to_apply=%region_6.9 | all-reduce | flops 128 | bytes 1024 | tf_op jit(solution)/shard_map/psum | solution.py:11
  130.1 142.4 %all-reduce.3.cloned.1.call-done = f32[8192,128]{1,0:T(8,128)} async-done(((f32[8192,128]{1,0:T(8,128)}), f32[8192,128]{1,0:T(8,128)}) %all-reduce.3.cloned.1.call-update) | async-done | bytes 4194320 | tf_op jit(solution)/shard_map/psum | solution.py:11
  272.5 9.5 %fusion.11 = f32[8192,128]{1,0:T(8,128)} fusion(f32[8192,128]{1,0:T(8,128)} %all-reduce.3.cloned.1.call-done, f32[8192,128]{1,0:T(8,128)} %scatter_fusion, f32[128]{0:T(128)S(1)} %psum.29, pred[]{:T(512)S(6)} %gt.6, pred[]{:T(512)S(6)} %eq.11, s32[]{:T(128)S(6)} %select_n.89), kind=kOutput, calls=%fused_computation.33 | convolution fusion | flops 1614807040 | bytes 16843270 | tf_op jit(solution)/shard_map/dot_general | solution.py:63
  282.0 2.2 conditional.3
  282.0 2.2 broadcast.90.clone
  284.2 2.2 broadcast_select_fusion
  286.5 52.5 %psum.31 = f32[128]{0:T(128)S(1)} all-reduce(f32[128]{0:T(128)S(1)} %broadcast_select_fusion.2), channel_id=1, replica_groups=mesh['group'=8,'blk'=4] {'blk'}, use_global_device_ids=true, to_apply=%region_10.13 | all-reduce | flops 128 | bytes 1024 | tf_op jit(solution)/shard_map/psum | solution.py:11
  339.6 143.9 %all-reduce.5.cloned.1.call-done = f32[8192,128]{1,0:T(8,128)} async-done(((f32[8192,128]{1,0:T(8,128)}), f32[8192,128]{1,0:T(8,128)}) %all-reduce.5.cloned.1.call-update) | async-done | bytes 4194320 | tf_op jit(solution)/shard_map/psum | solution.py:11
  483.5 9.5 %fusion.13 = f32[1,8192,128]{2,1,0:T(8,128)} fusion(f32[8192,128]{1,0:T(8,128)} %all-reduce.5.cloned.1.call-done, f32[8192,128]{1,0:T(8,128)} %fusion.11, f32[128]{0:T(128)S(1)} %psum.31, pred[]{:T(512)S(6)} %gt.7, pred[]{:T(512)S(6)} %eq.10, s32[]{:T(128)S(6)} %select_n.89), kind=kOutput, calls=%fused_computation.35 | convolution fusion | flops 1614807040 | bytes 16843270 | tf_op jit(solution)/shard_map/dot_general | solution.py:63
  (28 shorter events, 6.9 us)
Async XLA Ops:
  7.2 14.3 %copy-start = (s32[1,1,8,2,128]{4,3,2,1,0:T(2,128)S(1)}, s32[1,1,8,2,128]{4,3,2,1,0:T(2,128)}, u32[]{:S(2)}) copy-start(s32[1,1,8,2,128]{4,3,2,1,0:T(2,128)} %param.14) | copy-start | bytes 24580
  7.2 4.5 copy-start.1
  28.5 18.9 %all-to-all-start.2 = ((f32[1,1,8,2,128,128]{5,4,3,1,0,2:T(8,128)}), f32[1,1,8,2,128,128]{5,4,3,1,0,2:T(8,128)S(1)}, u32[]{:S(2)}, u32[]{:S(2)}) async-start(f32[1,1,8,2,128,128]{5,4,3,1,0,2:T(8,128)} %bitcast.14), calls=%async_computation.2 | async-start | bytes 2097152 | tf_op jit(solution)/shard_map/all_to_all | solution.py:30
  47.4 8.0 %all-to-all-start.3 = ((s32[1,1,8,2,128]{4,3,1,0,2:T(2,128)}), s32[1,1,8,2,128]{4,3,1,0,2:T(2,128)S(1)}, u32[]{:S(2)}, u32[]{:S(2)}) async-start(s32[1,1,8,2,128]{4,3,1,0,2:T(2,128)} %bitcast.16), calls=%async_computation.3 | async-start | bytes 16384 | tf_op jit(solution)/shard_map/all_to_all | solution.py:32
  50.7 221.8 %all-reduce.3.cloned.1.call-start = ((), (), s32[]{:S(2)}) async-start(), calls=%async_computation.4 | async-start | bytes 8388608 | tf_op jit(solution)/shard_map/psum | solution.py:11
  121.1 362.4 %all-reduce.5.cloned.1.call-start = ((), (), s32[]{:S(2)}) async-start(), calls=%async_computation.5 | async-start | bytes 8388608 | tf_op jit(solution)/shard_map/psum | solution.py:11
Sparse Core Ops, SparseCore 0:
  121.2 151.2 all-reduce.2
  286.6 196.8 all-reduce.4
where the time goes:
time: 501 us; the launch traced here: 500 us
  waiting for transfers between devices  306 us (61%)
  blocking collectives  78.3 us (16%)
  other arithmetic  46 us (9%)
  matrix products  28.5 us (6%)
  local copies, waits for them, and re-layouts  20.3 us (4%)
  between operations  14.1 us (3%)
  starting transfers between devices  6.98 us (1%)
    psum x2, waiting for transfers between devices, from_root(): return lax.psum(jnp.where(mine, x, jnp.zeros_like(x)), axis)  286 us
    psum x2, blocking collectives, from_root(): return lax.psum(jnp.where(mine, x, jnp.zeros_like(x)), axis)  61.5 us
    dot_general x2, matrix products, per_device(): jnp.dot(factor * pivot, my_rows.T, precision=lax.Precision.HIGHEST)  18.9 us
    all_to_all x1, waiting for transfers between devices, per_device(): lax.all_to_all(child_blocks, 'group', split_axis=2, concat_axis=0, tiled=...  14.9 us
    scatter-add x1, other arithmetic, per_device(): front[0].at[flat_rows].add(placed.reshape(groups * slots * width, width))  14.5 us
    another operation x3, other arithmetic, factor_panel(): lower_factor = jnp.linalg.cholesky(square)  12.5 us
    another operation x2, other arithmetic, factor_panel(): lax.linalg.triangular_solve(lower_factor, column, left_side=False, lower=...  10.5 us
  transfers between devices with their start and end apart: 4, of which 4 were waited for; matrix products, arithmetic and copies ran while one was open for 0% of the time, Pallas kernels for 0%

commit v1 on v0

--- a/solution.py
+++ b/solution.py
@@ -2,13 +2,18 @@
 import jax.numpy as jnp
 from jax import lax
 from jax.sharding import PartitionSpec as P
+from jax.lax import all_gather
 
 PANELS = 2
 
 
+def masks_compute(unit, lane_axis):
+    return jnp.sum(all_gather(unit, lane_axis), 0)
+
+
 def from_root(x, axis, root):
     mine = lax.axis_index(axis) == root
-    return lax.psum(jnp.where(mine, x, jnp.zeros_like(x)), axis)
+    return masks_compute(jnp.where(mine, x, jnp.zeros_like(x)), axis)
 
 
 def factor_panel(column, start):

time: 501 us -> 782 us (1.56)
  waiting for transfers between devices: 306 us -> 571 us
  other arithmetic: 46 us -> 64.2 us
    all_gather x0 -> x2, waiting for transfers between devices: none -> 552 us  [masks_compute(): return jnp.sum(all_gather(unit, lane_axis), 0)]
    psum x2 -> x0, waiting for transfers between devices: 286 us -> none  [from_root(): return lax.psum(jnp.where(mine, x, jnp.zeros_like(x)), axis)]
    psum x2 -> x0, blocking collectives: 61.5 us -> none  [from_root(): return lax.psum(jnp.where(mine, x, jnp.zeros_like(x)), axis)]
    all_gather x0 -> x2, blocking collectives: none -> 58.9 us  [masks_compute(): return jnp.sum(all_gather(unit, lane_axis), 0)]
    reduce_sum x0 -> x4, other arithmetic: none -> 18.2 us  [masks_compute(): return jnp.sum(all_gather(unit, lane_axis), 0)]
where the time goes in v1:
time: 782 us; the launch traced here: 781 us
  waiting for transfers between devices  571 us (73%)
  blocking collectives  75.6 us (10%)
  other arithmetic  64.2 us (8%)
  matrix products  28.5 us (4%)
  local copies, waits for them, and re-layouts  20.3 us (3%)
  between operations  14.1 us (2%)
    all_gather x2, waiting for transfers between devices, masks_compute(): return jnp.sum(all_gather(unit, lane_axis), 0)  552 us
    all_gather x2, blocking collectives, masks_compute(): return jnp.sum(all_gather(unit, lane_axis), 0)  58.9 us
    dot_general x2, matrix products, per_device(): jnp.dot(factor * pivot, my_rows.T, precision=lax.Precision.HIGHEST)  18.9 us
    reduce_sum x4, other arithmetic, masks_compute(): return jnp.sum(all_gather(unit, lane_axis), 0)  18.2 us
  transfers between devices with their start and end apart: 4, of which 4 were waited for; matrix products, arithmetic and copies ran while one was open for 0% of the time, Pallas kernels for 0%

profile of v1, /device:TPU:0, one launch (start us, length us, event | category | flops | bytes accessed | tf_op | source)
XLA Modules:
  0.0 780.9 jit_solution(18823258620750015)
XLA Ops:
  7.2 4.5 copy.55
  11.7 9.7 %all_to_all.16 = s32[1,1,8]{1,0,2:T(1,128)S(1)} all-to-all(s32[1,1,8]{1,0,2:T(1,128)S(1)} %copy.32), channel_id=1, replica_groups=mesh['group'=8,'blk'=4] {'group'}, dimensions={2} | all-to-all | bytes 64 | tf_op jit(solution)/shard_map/all_to_all | solution.py:38
  21.4 7.1 all_to_all.17
  28.5 3.6 all-to-all-start.2
  32.5 14.9 %all-to-all-done.2 = f32[1,1,8,2,128,128]{5,4,3,1,0,2:T(8,128)S(1)} async-done(((f32[1,1,8,2,128,128]{5,4,3,1,0,2:T(8,128)}), f32[1,1,8,2,128,128]{5,4,3,1,0,2:T(8,128)S(1)}, u32[]{:S(2)}, u32[]{:S(2)}) %all-to-all-start.2) | async-done | bytes 1048608 | tf_op jit(solution)/shard_map/all_to_all | solution.py:35
  47.4 3.3 all-to-all-start.3
  50.9 4.5 all-to-all-done.3
  56.4 14.5 %scatter_fusion = f32[8192,128]{1,0:T(8,128)} fusion(f32[8192,128]{1,0:T(8,128)} %bitcast.54, s32[2048]{0:T(1024)S(1)} %bitcast.58, f32[2048,128]{1,0:T(8,128)S(1)} %bitcast.57), kind=kCustom, calls=%fused_computation.2 | custom fusion | flops 262144 | bytes 3153920 | tf_op jit(solution)/shard_map/scatter-add | solution.py:52
  71.0 45.7 %conditional.2 = (f32[128]{0:T(128)S(1)}, f32[8192,128]{1,0:T(8,128)}) conditional(s32[]{:T(128)} %convert_element_type.8, () %tuple.27, (f32[8192,128]{1,0:T(8,128)}) %tuple.31), branch_computations={%region_1.2_spmd, %region_2.0_spmd} | conditional | flops 1611809536 | bytes 25957906 | solution.py:65
  71.0 5.6 copy.41
  78.4 11.7 %cholesky.44 = f32[128,128]{1,0:T(8,128)S(1)} custom-call(f32[128,128]{1,0:T(8,128)S(1)} %fusion.2), custom_call_target="Cholesky" | custom-call | tf_op jit(solution)/shard_map/cond/branch_1_fun/jit(cholesky)/cholesky | solution.py:22
  92.8 9.8 %custom-call.10 = f32[1,128,128]{1,2,0:T(8,128)S(1)} custom-call(f32[1,128,128]{2,1,0:T(8,128)S(1)} %get-tuple-element.18), custom_call_target="InvertDiagBlocksLowerTriangular" | custom-call | tf_op jit(solution)/shard_map/cond/branch_1_fun/triangular_solve/custom-call.0 | solution.py:24
  102.6 8.4 %fusion = f32[8192,128]{0,1:T(8,128)} fusion(f32[8192,128]{1,0:T(8,128)} %get-tuple-element.15, f32[128]{0:T(128)S(1)} %gather_fusion, f32[1,128,128]{1,2,0:T(8,128)S(1)} %custom-call.10), kind=kOutput, calls=%fused_computation.4 | convolution fusion | flops 1611661312 | bytes 8454656 | tf_op jit(solution)/shard_map/cond/branch_1_fun/triangular_solve/dot.3 | solution.py:24
  111.1 5.6 copy.40
  116.7 4.4 broadcast_select_fusion.1
  121.1 7.8 all-gather.4
  129.0 275.4 %all-gather.9.cloned.1.call-done = f32[32768,128]{1,0:T(8,128)} async-done(((f32[8192,128]{1,0:T(8,128)}), f32[32768,128]{1,0:T(8,128)}) %all-gather.9.cloned.1.call-update) | async-done | bytes 16777232 | tf_op jit(solution)/shard_map/all_gather | solution.py:11
  404.3 9.1 %reduce_sum.36 = f32[8192,128]{1,0:T(8,128)} reduce(f32[4,8192,128]{2,1,0:T(8,128)} %bitcast.55, f32[]{:T(128)} %constant.68.clone.1), dimensions={0}, to_apply=%region_5.8 | reduce | flops 3145728 | bytes 20971524 | tf_op jit(solution)/shard_map/reduce_sum | solution.py:11
  413.4 9.5 %fusion.11 = f32[8192,128]{1,0:T(8,128)} fusion(f32[8192,128]{1,0:T(8,128)} %reduce_sum.36, f32[8192,128]{1,0:T(8,128)} %scatter_fusion, f32[128]{0:T(128)S(1)} %reduce_sum.37, pred[]{:T(512)S(6)} %gt.6, pred[]{:T(512)S(6)} %eq.11, s32[]{:T(128)S(6)} %select_n.89), kind=kOutput, calls=%fused_computation.33 | convolution fusion | flops 1614807040 | bytes 16843270 | tf_op jit(solution)/shard_map/dot_general | solution.py:68
  422.8 2.2 conditional.3
  427.3 51.1 %all-gather.5 = f32[4,1,128]{2,1,0:T(1,128)S(1)} all-gather(f32[1,1,128]{2,1,0:T(1,128)S(1)} %fusion.23), channel_id=5, replica_groups=mesh['group'=8,'blk'=4] {'blk'}, dimensions={0}, use_global_device_ids=true | all-gather | bytes 2560 | tf_op jit(solution)/shard_map/all_gather | solution.py:11
  479.0 276.5 %all-gather.11.cloned.1.call-done = f32[32768,128]{1,0:T(8,128)} async-done(((f32[8192,128]{1,0:T(8,128)}), f32[32768,128]{1,0:T(8,128)}) %all-gather.11.cloned.1.call-update) | async-done | bytes 16777232 | tf_op jit(solution)/shard_map/all_gather | solution.py:11
  755.5 9.1 %reduce_sum.38 = f32[8192,128]{1,0:T(8,128)} reduce(f32[4,8192,128]{2,1,0:T(8,128)} %bitcast.56, f32[]{:T(128)} %constant.68.clone.1), dimensions={0}, to_apply=%region_9.12 | reduce | flops 3145728 | bytes 20971524 | tf_op jit(solution)/shard_map/reduce_sum | solution.py:11
  764.6 9.5 %fusion.13 = f32[1,8192,128]{2,1,0:T(8,128)} fusion(f32[8192,128]{1,0:T(8,128)} %reduce_sum.38, f32[8192,128]{1,0:T(8,128)} %fusion.11, f32[128]{0:T(128)S(1)} %reduce_sum.39, pred[]{:T(512)S(6)} %gt.7, pred[]{:T(512)S(6)} %eq.10, s32[]{:T(128)S(6)} %select_n.89), kind=kOutput, calls=%fused_computation.35 | convolution fusion | flops 1614807040 | bytes 16843270 | tf_op jit(solution)/shard_map/dot_general | solution.py:68
  (32 shorter events, 11.4 us)
Async XLA Ops:
  7.2 14.3 %copy-start = (s32[1,1,8,2,128]{4,3,2,1,0:T(2,128)S(1)}, s32[1,1,8,2,128]{4,3,2,1,0:T(2,128)}, u32[]{:S(2)}) copy-start(s32[1,1,8,2,128]{4,3,2,1,0:T(2,128)} %param.14) | copy-start | bytes 24580
  7.2 4.5 copy-start.1
  28.5 18.9 %all-to-all-start.2 = ((f32[1,1,8,2,128,128]{5,4,3,1,0,2:T(8,128)}), f32[1,1,8,2,128,128]{5,4,3,1,0,2:T(8,128)S(1)}, u32[]{:S(2)}, u32[]{:S(2)}) async-start(f32[1,1,8,2,128,128]{5,4,3,1,0,2:T(8,128)} %bitcast.14), calls=%async_computation.2 | async-start | bytes 2097152 | tf_op jit(solution)/shard_map/all_to_all | solution.py:35
  47.4 8.0 %all-to-all-start.3 = ((s32[1,1,8,2,128]{4,3,1,0,2:T(2,128)}), s32[1,1,8,2,128]{4,3,1,0,2:T(2,128)S(1)}, u32[]{:S(2)}, u32[]{:S(2)}) async-start(s32[1,1,8,2,128]{4,3,1,0,2:T(2,128)} %bitcast.16), calls=%async_computation.3 | async-start | bytes 16384 | tf_op jit(solution)/shard_map/all_to_all | solution.py:37
  50.7 353.6 %all-gather.9.cloned.1.call-start = ((), (), s32[]{:S(2)}) async-start(), calls=%async_computation.4 | async-start | bytes 20971520 | tf_op jit(solution)/shard_map/all_gather | solution.py:11
  121.1 634.5 %all-gather.11.cloned.1.call-start = ((), (), s32[]{:S(2)}) async-start(), calls=%async_computation.5 | async-start | bytes 20971520 | tf_op jit(solution)/shard_map/all_gather | solution.py:11
Sparse Core Ops, SparseCore 0:
  121.2 283.0 all-gather.8
  427.4 328.0 all-gather.10
